TPU v7x, 32 devices: a whole 2x2x4 slice. The times are simulated.
32 devices in a mesh: groups: 2 (over y), blk: 4 (over z), oct: 2 (over x), sub: 2 (over core).
Axes of the slice: x: 2, y: 2, z: 4, core: 2. Of those that a mesh axis runs over, the one named last changes fastest.
Arguments:
- positions: float32 [3, 65536], P(None, ('groups', 'blk', 'oct', 'sub')), parts along dimension 1, may hold values from 0 to 320
- polarizability: float32 [65536], P(('groups', 'blk', 'oct', 'sub')), parts along dimension 0, may hold values from 0.5 to 1.5
- permanent_field: float32 [3, 65536], P(None, ('groups', 'blk', 'oct', 'sub')), parts along dimension 1, may hold values from -40 to 40
- group_id: int32 [65536], P(('groups', 'blk', 'oct', 'sub')), parts along dimension 0, may hold values from 0 to 10921, never falling along the last dimension, each value on 1 to 6 neighbouring positions
- pair_mask: int32 [512, 9], P(('groups', 'blk', 'oct', 'sub')), parts along dimension 0, may hold values from 0 to 1, as said below
Outputs:
- dipoles: float32 [3, 65536], P(None, ('groups', 'blk', 'oct', 'sub')), parts along dimension 1
- residual: float32 [3, 65536], P(None, ('groups', 'blk', 'oct', 'sub')), parts along dimension 1
There are 2 independent parts, one for each index of `groups`. A program takes and returns all parts, laid end to end along the dimension named above; each array names one. Nothing has to cross between parts.
Inputs may be any that keep to these rules, and one draw needn't show every extreme that they name: `group_id`: never falls from one atom to the next; each value names 1 to 6 consecutive atoms. pair_mask[b, 4] = 1, and pair_mask[b, 4 + o] = pair_mask[(b + o) mod 256, 4 - o].
All inputs are finite; a program needn't handle non-finite values.
Results may differ from a plain program's by a relative error of at most 0.0003.
Values sent between devices are 32-bit elements; how exact they have to be, the bound alone decides.
No kernel may reach another device: no remote copies, remote signals or barrier semaphores. Data moves between devices by JAX's collectives and lax.ppermute only.
A program may use at most 64 MiB of HBM per device.

v0:
```python
import math
import jax
import jax.numpy as jnp
import numpy as np
from jax import lax
from jax.sharding import PartitionSpec as P

BOXES_DEV = 2
BLOCK = 128
ORDER = 5
NODE_PAD = 128
ITERS = 2
side_length = 32.0
layer_gap = 2.5
thole_damp = 0.39
highest = lax.Precision.HIGHEST


def padded(cells, sides, width):
    for axis, dim in sides:
        count = lax.axis_size(axis)
        head = lax.slice_in_dim(cells, 0, width, axis=dim)
        tail = lax.slice_in_dim(cells, cells.shape[dim] - width, cells.shape[dim], axis=dim)
        cells = jnp.concatenate(
            [
                lax.ppermute(tail, axis, [(i, (i + 1) % count) for i in range(count)]),
                cells,
                lax.ppermute(head, axis, [((i + 1) % count, i) for i in range(count)]),
            ],
            axis=dim,
        )
    return cells


def wrap_image(delta, period):
    return delta - period * jnp.floor(delta / period + 0.5)


def split_size(total, limit):
    best = 1
    for factor in range(1, min(total, limit) + 1):
        if total % factor == 0:
            best = factor
    return best


def near_tiles(target, source, moments, keep_tile, length_z):
    delta_x = wrap_image(target[0][:, :, None] - source[0][:, None, :], side_length)
    delta_y = wrap_image(target[1][:, :, None] - source[1][:, None, :], side_length)
    delta_z = wrap_image(target[2][:, :, None] - source[2][:, None, :], length_z)
    keep = (keep_tile[:, None, None] > 0.5) & (target[4][:, :, None] != source[4][:, None, :])
    dist_sq = jnp.where(keep, delta_x * delta_x + delta_y * delta_y + delta_z * delta_z, 1.0)
    inv_three = lax.rsqrt(dist_sq) / dist_sq
    scaled = (
        thole_damp
        * dist_sq
        * jnp.sqrt(dist_sq)
        * lax.rsqrt(target[3][:, :, None] * source[3][:, None, :])
    )
    lam_three = -jnp.expm1(-scaled)
    lam_five = lam_three - scaled * jnp.exp(-scaled)
    coef_five = jnp.where(keep, 3.0 * lam_five * inv_three / dist_sq, 0.0)
    coef_three = jnp.where(keep, lam_three * inv_three, 0.0)
    along = (
        delta_x * moments[0][:, None, :]
        + delta_y * moments[1][:, None, :]
        + delta_z * moments[2][:, None, :]
    )
    weighted = coef_five * along
    field_x = jnp.sum(weighted * delta_x - coef_three * moments[0][:, None, :], axis=2)
    field_y = jnp.sum(weighted * delta_y - coef_three * moments[1][:, None, :], axis=2)
    field_z = jnp.sum(weighted * delta_z - coef_three * moments[2][:, None, :], axis=2)
    return jnp.stack([field_x, field_y, field_z])


def near_total(static_ext, dipole_ext, mask_rows, length_z, atom_count):
    reach = (mask_rows.shape[1] - 1) // 2
    width = reach * BLOCK
    blocks = atom_count // BLOCK
    target = static_ext[:, width : width + atom_count].reshape(5, blocks, BLOCK)
    total = jnp.zeros((3, blocks, BLOCK), static_ext.dtype)
    for offset in range(-reach, reach + 1):
        begin = (reach + offset) * BLOCK
        source = static_ext[:, begin : begin + atom_count].reshape(5, blocks, BLOCK)
        moments = dipole_ext[:, begin : begin + atom_count].reshape(3, blocks, BLOCK)
        keep_tile = mask_rows[:, reach + offset].astype(static_ext.dtype)
        total = total + near_tiles(target, source, moments, keep_tile, length_z)
    return total.reshape(3, atom_count)


def node_tables():
    count = ORDER
    roots = np.cos((2.0 * np.arange(count) + 1.0) * np.pi / (2.0 * count))
    degree = np.arange(count)
    coeff = (
        2.0 / count * np.cos(np.outer(2.0 * np.arange(count) + 1.0, degree) * np.pi / (2.0 * count))
    )
    coeff = np.where(degree[None, :] == 0, 1.0 / count, coeff)
    index = np.arange(NODE_PAD)
    live = index < count**3
    safe = np.where(live, index, 0)
    first = safe // (count * count)
    second = safe // count % count
    third = safe % count
    levels = np.arange(count)[None, :]
    pick_a = (first[:, None] == levels) * live[:, None] * 1.0
    pick_b = (second[:, None] == levels) * 1.0
    pick_c = (third[:, None] == levels) * 1.0
    node_x = 16.0 * (1.0 + roots[first])
    node_y = 16.0 * (1.0 + roots[second])
    node_t = roots[third]
    tables = [coeff, pick_a, pick_b, pick_c, node_x, node_y, node_t]
    return [jnp.asarray(item, jnp.float32) for item in tables]


def interpolation(coords, box_ids, box_height):
    coeff, pick_a, pick_b, pick_c, node_x, node_y, node_t = node_tables()
    scaled_x = coords[0] / 16.0 - 1.0
    scaled_y = coords[1] / 16.0 - 1.0
    scaled_z = (
        2.0 * (coords[2] - box_ids.astype(coords.dtype)[:, None] * box_height) / box_height - 1.0
    )

    def basis(values, picks):
        terms = [jnp.ones_like(values), values]
        for degree in range(2, ORDER):
            terms.append(2.0 * values * terms[-1] - terms[-2])
        stacked = jnp.stack(terms[:ORDER])
        smooth = jnp.einsum("kn,nba->kba", coeff, stacked, precision=highest)
        return jnp.einsum("pk,kba->pba", picks, smooth, precision=highest)

    return basis(scaled_x, pick_a) * basis(scaled_y, pick_b) * basis(scaled_z, pick_c)


def far_block(target_ids, source_ids, weights, slabs, box_height, length_z):
    coeff, pick_a, pick_b, pick_c, node_x, node_y, node_t = node_tables()
    height_t = (
        target_ids.astype(weights.dtype)[:, None] * box_height
        + 0.5 * box_height * (1.0 + node_t)[None, :]
    )
    height_s = (
        source_ids.astype(weights.dtype)[:, None] * box_height
        + 0.5 * box_height * (1.0 + node_t)[None, :]
    )
    delta_x = wrap_image(node_x[:, None] - node_x[None, :], side_length)[None, :, None, :]
    delta_y = wrap_image(node_y[:, None] - node_y[None, :], side_length)[None, :, None, :]
    delta_z = wrap_image(height_t[:, :, None, None] - height_s[None, None, :, :], length_z)
    apart = jnp.abs(target_ids[:, None] // BOXES_DEV - source_ids[None, :] // BOXES_DEV)
    apart = jnp.minimum(apart, slabs - apart)
    keep = (apart >= 1)[:, None, :, None]
    dist_sq = jnp.where(
        keep,
        delta_x * delta_x + delta_y * delta_y + delta_z * delta_z + box_height * box_height,
        1.0,
    )
    inv_three = lax.rsqrt(dist_sq) / dist_sq
    coef_five = jnp.where(keep, 3.0 * inv_three / dist_sq, 0.0)
    coef_three = jnp.where(keep, inv_three, 0.0)
    weight_x = weights[:, 0, :][None, None]
    weight_y = weights[:, 1, :][None, None]
    weight_z = weights[:, 2, :][None, None]
    weighted = coef_five * (delta_x * weight_x + delta_y * weight_y + delta_z * weight_z)
    field_x = jnp.sum(weighted * delta_x - coef_three * weight_x, axis=(2, 3))
    field_y = jnp.sum(weighted * delta_y - coef_three * weight_y, axis=(2, 3))
    field_z = jnp.sum(weighted * delta_z - coef_three * weight_z, axis=(2, 3))
    return jnp.stack([field_x, field_y, field_z], axis=1)


def on_device(positions, polarizability, permanent_field, group_id, pair_mask):
    slabs = lax.axis_size(("blk", "oct", "sub"))
    member = lax.axis_index(("blk", "oct", "sub"))
    atom_count = positions.shape[1]
    length_z = layer_gap * atom_count * slabs / 256.0
    box_height = length_z / (BOXES_DEV * slabs)
    per_box = atom_count // BOXES_DEV
    width = (pair_mask.shape[1] - 1) // 2 * BLOCK
    group_limit = max(1, 32 // BOXES_DEV)
    static = jnp.concatenate(
        [positions, polarizability[None, :], group_id.astype(jnp.float32)[None, :]], axis=0
    )
    static_ext = padded(static, ((("blk", "oct", "sub"), 1),), width)
    own_boxes = member * BOXES_DEV + jnp.arange(BOXES_DEV, dtype=jnp.int32)
    interp = interpolation(positions.reshape(3, BOXES_DEV, per_box), own_boxes, box_height)
    surface = 4.0 * math.pi / 3.0 / (side_length * side_length * length_z)

    def induced(dipoles, total):
        dipole_ext = padded(dipoles, ((("blk", "oct", "sub"), 1),), width)
        near = near_total(static_ext, dipole_ext, pair_mask, length_z, atom_count)
        weights = jnp.einsum(
            "pba,cba->bcp", interp, dipoles.reshape(3, BOXES_DEV, per_box), precision=highest
        )
        piece = lax.all_gather(weights, ("blk", "oct", "sub"), axis=0, tiled=True)
        start = jnp.int32(0)
        count = piece.shape[0]
        size = split_size(count, group_limit)
        grouped = piece.reshape(count // size, size, 3, piece.shape[2])

        def visit(acc, item):
            index, bundle = item
            sources = start + index * size + jnp.arange(size, dtype=jnp.int32)
            return (acc + far_block(own_boxes, sources, bundle, slabs, box_height, length_z), None)

        result, unused = lax.scan(
            visit, jnp.zeros_like(weights), (jnp.arange(count // size, dtype=jnp.int32), grouped)
        )
        far = jnp.einsum("pba,bcp->cba", interp, result, precision=highest).reshape(3, atom_count)
        return near + far - surface * total[:, None]

    def moment(values):
        return lax.psum(jnp.sum(values, axis=1), ("blk", "oct", "sub"))

    def squares(resid, scaled):
        return lax.psum(jnp.sum(resid * scaled), ("blk", "oct", "sub"))

    dipoles = polarizability[None, :] * permanent_field
    residual = induced(dipoles, moment(dipoles))
    precond = polarizability[None, :] * residual
    direction = precond
    norm_now = squares(residual, precond)
    for step in range(ITERS):
        image = direction / polarizability[None, :] - induced(direction, moment(direction))
        rate = norm_now / lax.psum(jnp.sum(direction * image), ("blk", "oct", "sub"))
        dipoles = dipoles + rate * direction
        residual = residual - rate * image
        if step + 1 < ITERS:
            precond = polarizability[None, :] * residual
            norm_next = squares(residual, precond)
            direction = precond + norm_next / norm_now * direction
            norm_now = norm_next
    return (dipoles, residual)


def solution(mesh):
    return jax.shard_map(
        on_device,
        mesh=mesh,
        in_specs=(
            P(None, ("groups", "blk", "oct", "sub")),
            P(("groups", "blk", "oct", "sub")),
            P(None, ("groups", "blk", "oct", "sub")),
            P(("groups", "blk", "oct", "sub")),
            P(("groups", "blk", "oct", "sub"), None),
        ),
        out_specs=(
            P(None, ("groups", "blk", "oct", "sub")),
            P(None, ("groups", "blk", "oct", "sub")),
        ),
        check_vma=False,
    )
```

profile of v0, /device:TPU:0, one launch (start us, length us, event | category | flops | bytes accessed | tf_op | source)
XLA Modules:
  0.0 428.3 jit_solution(15247812564218952183)
XLA Ops:
  2.6 5.0 %collective-permute-start.2 = (f32[5,512]{1,0:T(8,128)S(1)}, f32[5,512]{1,0:T(8,128)S(1)}, u32[]{:S(2)}, u32[]{:S(2)}) collective-permute-start(f32[5,512]{1,0:T(8,128)S(1)} %get-tuple-element.990), channel_id=1, source_target_pairs={{1,0},{2,1},{3,2},{4,3},{5,4},{6,5},{7,6},{8,7},{9,8},{10,9},{11,1... | collective-permute-start | bytes 30728 | tf_op jit(solution)/shard_map/ppermute | solution.py:28
  8.6 4.4 %collective-permute-start.3 = (f32[3,512]{1,0:T(4,128)S(1)}, f32[3,512]{1,0:T(4,128)S(1)}, u32[]{:S(2)}, u32[]{:S(2)}) collective-permute-start(f32[3,512]{1,0:T(4,128)S(1)} %get-tuple-element.1086), channel_id=1, source_target_pairs={{1,0},{2,1},{3,2},{4,3},{5,4},{6,5},{7,6},{8,7},{9,8},{10,9},{11,1... | collective-permute-start | bytes 18440 | tf_op jit(solution)/shard_map/ppermute | solution.py:28
  14.0 29.5 %psum.49 = f32[3]{0:T(128)S(1)} all-reduce(f32[3]{0:T(128)S(1)} %get-tuple-element.927), channel_id=1, replica_groups=mesh['groups'=2,'blk'=4,'oct'=2,'sub'=2] {'blk','oct','sub'}, use_global_device_ids=true, to_apply=%region_33.34 | all-reduce | flops 3 | bytes 24 | tf_op jit(solution)/shard_map/psum | solution.py:210
  47.7 1.8 convolution_multiply_fusion.1
  49.6 1.8 fusion.90
  52.0 17.8 %all_gather.9 = f32[32,3,128]{2,1,0:T(4,128)S(1)} all-gather(f32[2,3,128]{2,1,0:T(4,128)S(1)} %fusion.782), channel_id=1, replica_groups=mesh['groups'=2,'blk'=4,'oct'=2,'sub'=2] {'blk','oct','sub'}, dimensions={0}, use_global_device_ids=true | all-gather | bytes 52224 | tf_op jit(solution)/shard_map/all_gather | solution.py:192
  69.9 13.5 %while.51 = (s32[]{:T(128)}, f32[2,3,128]{2,0,1:T(2,128)S(1)}, s32[2]{0:T(128)S(1)}, f32[2,16,3,128]{3,1,2,0:T(8,128)S(1)}, s32[]{:T(128)}, /*index=5*/s32[]{:T(...) while((s32[]{:T(128)}, f32[2,3,128]{2,0,1:T(2,128)S(1)}, ...), condition=%wide.region_31.32_spmd.clone.clone.clone.clone, body=%wide.region_27.31_spmd.sunk.clone.clone.clone.clone.sunk | while | flops 16765948 | bytes 2795035 | solution.py:203
  71.8 4.8 %subtract_reduce_fusion.9 = (f32[2,128]{1,0:T(2,128)S(1)}, f32[2,128]{1,0:T(2,128)S(1)}, f32[2,128]{1,0:T(2,128)S(1)}) fusion(f32[16,128]{1,0:T(8,128)S(1)} %get-tuple-element.1216, f32[128,128]{1,0:T(8,128)S(1)} %get-tuple-element.1217, pred[2,16]{1,0:T(4,128)(4,1)S(1)} %fusion.814, f32[16,128]{1,0:T(8,128)S(1)} %broadcast_add_fusion.12, ...), kind=kLoop, calls=%fused_computation.28.clone.1 | loop fusion | flops 15727872 | bytes 1282080 | tf_op jit(solution)/shard_map/while/body/eval_jaxpr/reduce_sum | solution.py:163
  78.5 4.8 %subtract_reduce_fusion.9 = (f32[2,128]{1,0:T(2,128)S(1)}, f32[2,128]{1,0:T(2,128)S(1)}, f32[2,128]{1,0:T(2,128)S(1)}) fusion(f32[16,128]{1,0:T(8,128)S(1)} %get-tuple-element.1216, f32[128,128]{1,0:T(8,128)S(1)} %get-tuple-element.1217, pred[2,16]{1,0:T(4,128)(4,1)S(1)} %fusion.814, f32[16,128]{1,0:T(8,128)S(1)} %broadcast_add_fusion.12, ...), kind=kLoop, calls=%fused_computation.28.clone.1 | loop fusion | flops 15727872 | bytes 1282080 | tf_op jit(solution)/shard_map/while/body/eval_jaxpr/reduce_sum | solution.py:163
  84.2 4.0 fusion.558
  88.2 4.0 fusion.585
  92.2 4.0 fusion.567
  96.2 4.0 fusion.576
  100.2 4.0 fusion.603
  104.2 4.0 fusion.621
  108.2 4.0 fusion.612
  112.2 7.3 %fusion.630 = (f32[16,128]{1,0:T(8,128)S(1)}, f32[16,128]{1,0:T(8,128)S(1)}, f32[16,128]{1,0:T(8,128)S(1)}, f32[16,128]{1,0:T(8,128)S(1)}, f32[16,128]{1,0:T(8,128)S(1)}, /*index=5*/f32[16,128]{1,0:T(8,128)S(1)}) fusion(f32[16,128]{1,0:T(8,128)S(1)} %bitcast.840, f32[16,128]{1,0:T(8,128)S(1)} %bitcast.735, f32[16,128]{1,0:T(8,128)S(1)} %bitcast.931, ...), kind=kLoop, calls=%fused_computation.815 | loop fusion | flops 30920704 | bytes 180256 | tf_op jit(solution)/shard_map/reduce_sum | solution.py:70
  120.7 31.6 %psum.51 = f32[3]{0:T(128)S(1)} all-reduce(f32[3]{0:T(128)S(1)} %get-tuple-element.923), channel_id=1, replica_groups=mesh['groups'=2,'blk'=4,'oct'=2,'sub'=2] {'blk','oct','sub'}, use_global_device_ids=true, to_apply=%region_69.70 | all-reduce | flops 3 | bytes 24 | tf_op jit(solution)/shard_map/psum | solution.py:210
  153.2 4.4 %collective-permute-start.5 = (f32[3,512]{1,0:T(4,128)S(1)}, f32[3,512]{1,0:T(4,128)S(1)}, u32[]{:S(2)}, u32[]{:S(2)}) collective-permute-start(f32[3,512]{1,0:T(4,128)S(1)} %get-tuple-element.1078), channel_id=1, source_target_pairs={{1,0},{2,1},{3,2},{4,3},{5,4},{6,5},{7,6},{8,7},{9,8},{10,9},{11,1... | collective-permute-start | bytes 18440 | tf_op jit(solution)/shard_map/ppermute | solution.py:28
  157.6 17.3 %all_gather.10 = f32[32,3,128]{2,1,0:T(4,128)S(1)} all-gather(f32[2,3,128]{2,1,0:T(4,128)S(1)} %fusion.684), channel_id=1, replica_groups=mesh['groups'=2,'blk'=4,'oct'=2,'sub'=2] {'blk','oct','sub'}, dimensions={0}, use_global_device_ids=true | all-gather | bytes 52224 | tf_op jit(solution)/shard_map/all_gather | solution.py:192
  174.9 13.0 %while.52 = (s32[]{:T(128)}, f32[2,3,128]{2,0,1:T(2,128)S(1)}, s32[2]{0:T(128)S(1)}, f32[2,16,3,128]{3,1,2,0:T(8,128)S(1)}, s32[]{:T(128)}, /*index=5*/s32[]{:T(...) while((s32[]{:T(128)}, f32[2,3,128]{2,0,1:T(2,128)S(1)}, ...), condition=%wide.region_67.68_spmd.clone.clone.clone.clone, body=%wide.region_63.67_spmd.sunk.clone.clone.clone.clone.sunk | while | flops 16765948 | bytes 2795035 | solution.py:203
  176.6 4.8 %subtract_reduce_fusion.10 = (f32[2,128]{1,0:T(2,128)S(1)}, f32[2,128]{1,0:T(2,128)S(1)}, f32[2,128]{1,0:T(2,128)S(1)}) fusion(f32[16,128]{1,0:T(8,128)S(1)} %get-tuple-element.1230, f32[128,128]{1,0:T(8,128)S(1)} %get-tuple-element.1231, pred[2,16]{1,0:T(4,128)(4,1)S(1)} %fusion.817, f32[16,128]{1,0:T(8,128)S(1)} %broadcast_add_fusion.14, ...), kind=kLoop, calls=%fused_computation.82.clone.1 | loop fusion | flops 15727872 | bytes 1282080 | tf_op jit(solution)/shard_map/while/body/eval_jaxpr/reduce_sum | solution.py:163
  183.1 4.8 %subtract_reduce_fusion.10 = (f32[2,128]{1,0:T(2,128)S(1)}, f32[2,128]{1,0:T(2,128)S(1)}, f32[2,128]{1,0:T(2,128)S(1)}) fusion(f32[16,128]{1,0:T(8,128)S(1)} %get-tuple-element.1230, f32[128,128]{1,0:T(8,128)S(1)} %get-tuple-element.1231, pred[2,16]{1,0:T(4,128)(4,1)S(1)} %fusion.817, f32[16,128]{1,0:T(8,128)S(1)} %broadcast_add_fusion.14, ...), kind=kLoop, calls=%fused_computation.82.clone.1 | loop fusion | flops 15727872 | bytes 1282080 | tf_op jit(solution)/shard_map/while/body/eval_jaxpr/reduce_sum | solution.py:163
  188.0 4.0 fusion.602
  192.0 4.0 fusion.575
  196.1 4.0 fusion.566
  200.1 4.0 fusion.557
  204.1 4.0 fusion.584
  208.1 4.0 fusion.611
  212.1 4.0 fusion.620
  216.1 7.3 %fusion.629 = (f32[16,128]{1,0:T(8,128)S(1)}, f32[16,128]{1,0:T(8,128)S(1)}, f32[16,128]{1,0:T(8,128)S(1)}, f32[16,128]{1,0:T(8,128)S(1)}, f32[16,128]{1,0:T(8,128)S(1)}, /*index=5*/f32[16,128]{1,0:T(8,128)S(1)}) fusion(f32[16,128]{1,0:T(8,128)S(1)} %bitcast.872, f32[16,128]{1,0:T(8,128)S(1)} %bitcast.736, f32[16,128]{1,0:T(8,128)S(1)} %bitcast.939, ...), kind=kLoop, calls=%fused_computation.814 | loop fusion | flops 30920704 | bytes 180256 | tf_op jit(solution)/shard_map/reduce_sum | solution.py:70
  225.1 32.1 %all-reduce = (f32[]{:T(128)}, f32[]{:T(128)}) all-reduce(f32[]{:T(128)} %get-tuple-element.870, f32[]{:T(128)} %get-tuple-element.869), channel_id=1, replica_groups=mesh['groups'=2,'blk'=4,'oct'=2,'sub'=2] {'blk','oct','sub'}, use_global_device_ids=true, to_apply=%region_35.36 | all-reduce | flops 2 | bytes 16 | tf_op jit(solution)/shard_map/psum | solution.py:213
  259.1 30.1 %psum.53 = f32[]{:T(128)} all-reduce(f32[]{:T(128)} %fusion.632), channel_id=1, replica_groups=mesh['groups'=2,'blk'=4,'oct'=2,'sub'=2] {'blk','oct','sub'}, use_global_device_ids=true, to_apply=%region_73.74 | all-reduce | flops 1 | bytes 8 | tf_op jit(solution)/shard_map/psum | solution.py:213
  290.6 29.7 %psum.54 = f32[3]{0:T(128)S(1)} all-reduce(f32[3]{0:T(128)S(1)} %get-tuple-element.918), channel_id=1, replica_groups=mesh['groups'=2,'blk'=4,'oct'=2,'sub'=2] {'blk','oct','sub'}, use_global_device_ids=true, to_apply=%region_107.108 | all-reduce | flops 3 | bytes 24 | tf_op jit(solution)/shard_map/psum | solution.py:210
  321.3 4.4 %collective-permute-start.7 = (f32[3,512]{1,0:T(4,128)S(1)}, f32[3,512]{1,0:T(4,128)S(1)}, u32[]{:S(2)}, u32[]{:S(2)}) collective-permute-start(f32[3,512]{1,0:T(4,128)S(1)} %get-tuple-element.1070), channel_id=1, source_target_pairs={{1,0},{2,1},{3,2},{4,3},{5,4},{6,5},{7,6},{8,7},{9,8},{10,9},{11,1... | collective-permute-start | bytes 18440 | tf_op jit(solution)/shard_map/ppermute | solution.py:28
  325.7 17.3 %all_gather.11 = f32[32,3,128]{2,1,0:T(4,128)S(1)} all-gather(f32[2,3,128]{2,1,0:T(4,128)S(1)} %fusion.783), channel_id=1, replica_groups=mesh['groups'=2,'blk'=4,'oct'=2,'sub'=2] {'blk','oct','sub'}, dimensions={0}, use_global_device_ids=true | all-gather | bytes 52224 | tf_op jit(solution)/shard_map/all_gather | solution.py:192
  343.0 13.0 %while.53 = (s32[]{:T(128)}, f32[2,3,128]{2,0,1:T(2,128)S(1)}, s32[2]{0:T(128)S(1)}, f32[2,16,3,128]{3,1,2,0:T(8,128)S(1)}, s32[]{:T(128)}, /*index=5*/s32[]{:T(...) while((s32[]{:T(128)}, f32[2,3,128]{2,0,1:T(2,128)S(1)}, ...), condition=%wide.region_105.106_spmd.clone.clone.clone.clone, body=%wide.region_101.105_spmd.sunk.clone.clone.clone.clone.sunk | while | flops 16765948 | bytes 2795035 | solution.py:203
  344.7 4.8 %subtract_reduce_fusion.11 = (f32[2,128]{1,0:T(2,128)S(1)}, f32[2,128]{1,0:T(2,128)S(1)}, f32[2,128]{1,0:T(2,128)S(1)}) fusion(f32[16,128]{1,0:T(8,128)S(1)} %get-tuple-element.1244, f32[128,128]{1,0:T(8,128)S(1)} %get-tuple-element.1245, pred[2,16]{1,0:T(4,128)(4,1)S(1)} %fusion.820, f32[16,128]{1,0:T(8,128)S(1)} %broadcast_add_fusion.16, ...), kind=kLoop, calls=%fused_computation.136.clone.1 | loop fusion | flops 15727872 | bytes 1282080 | tf_op jit(solution)/shard_map/while/body/eval_jaxpr/reduce_sum | solution.py:163
  351.2 4.8 %subtract_reduce_fusion.11 = (f32[2,128]{1,0:T(2,128)S(1)}, f32[2,128]{1,0:T(2,128)S(1)}, f32[2,128]{1,0:T(2,128)S(1)}) fusion(f32[16,128]{1,0:T(8,128)S(1)} %get-tuple-element.1244, f32[128,128]{1,0:T(8,128)S(1)} %get-tuple-element.1245, pred[2,16]{1,0:T(4,128)(4,1)S(1)} %fusion.820, f32[16,128]{1,0:T(8,128)S(1)} %broadcast_add_fusion.16, ...), kind=kLoop, calls=%fused_computation.136.clone.1 | loop fusion | flops 15727872 | bytes 1282080 | tf_op jit(solution)/shard_map/while/body/eval_jaxpr/reduce_sum | solution.py:163
  356.1 4.0 fusion.556
  360.1 4.0 fusion.601
  364.2 4.0 fusion.565
  368.2 4.0 fusion.574
  372.2 4.0 fusion.583
  376.2 4.0 fusion.610
  380.3 4.0 fusion.619
  384.3 7.3 %fusion.628 = (f32[16,128]{1,0:T(8,128)S(1)}, f32[16,128]{1,0:T(8,128)S(1)}, f32[16,128]{1,0:T(8,128)S(1)}, f32[16,128]{1,0:T(8,128)S(1)}, f32[16,128]{1,0:T(8,128)S(1)}, /*index=5*/f32[16,128]{1,0:T(8,128)S(1)}) fusion(f32[16,128]{1,0:T(8,128)S(1)} %bitcast.862, f32[16,128]{1,0:T(8,128)S(1)} %bitcast.737, f32[16,128]{1,0:T(8,128)S(1)} %bitcast.947, ...), kind=kLoop, calls=%fused_computation.813 | loop fusion | flops 30920704 | bytes 180256 | tf_op jit(solution)/shard_map/reduce_sum | solution.py:70
  393.2 32.0 %psum.55 = f32[]{:T(128)} all-reduce(f32[]{:T(128)} %get-tuple-element.1104), channel_id=1, replica_groups=mesh['groups'=2,'blk'=4,'oct'=2,'sub'=2] {'blk','oct','sub'}, use_global_device_ids=true, to_apply=%region_109.110 | all-reduce | flops 1 | bytes 8 | tf_op jit(solution)/shard_map/psum | solution.py:222
  (174 shorter events, 24.9 us)
Async XLA Ops:
  0.6 45.0 %copy-start.8 = (f32[5,5,1]{1,0,2:T(8,128)S(1)}, f32[5,5,1]{1,0,2:T(8,128)}, u32[]{:S(2)}) copy-start(f32[5,5,1]{1,0,2:T(8,128)} %constant.532) | copy-start | bytes 304
  0.6 45.2 %copy-start.11 = (f32[128,5,1]{0,1,2:T(8,128)S(1)}, f32[128,5,1]{0,1,2:T(8,128)}, u32[]{:S(2)}) copy-start(f32[128,5,1]{0,1,2:T(8,128)} %constant.533) | copy-start | bytes 7684
  2.1 81.8 %collective-permute-start = (f32[5,512]{1,0:T(8,128)S(1)}, f32[5,512]{1,0:T(8,128)S(1)}, u32[]{:S(2)}, u32[]{:S(2)}) collective-permute-start(f32[5,512]{1,0:T(8,128)S(1)} %get-tuple-element.989), channel_id=1, source_target_pairs={{0,1},{1,2},{2,3},{3,4},{4,5},{5,6},{6,7},{7,8},{8,9},{9,10},{10,1... | collective-permute-start | bytes 30728 | tf_op jit(solution)/shard_map/ppermute | solution.py:26
  2.6 81.3 %collective-permute-start.2 = (f32[5,512]{1,0:T(8,128)S(1)}, f32[5,512]{1,0:T(8,128)S(1)}, u32[]{:S(2)}, u32[]{:S(2)}) collective-permute-start(f32[5,512]{1,0:T(8,128)S(1)} %get-tuple-element.990), channel_id=1, source_target_pairs={{1,0},{2,1},{3,2},{4,3},{5,4},{6,5},{7,6},{8,7},{9,8},{10,9},{11,1... | collective-permute-start | bytes 30728 | tf_op jit(solution)/shard_map/ppermute | solution.py:28
  8.6 75.2 %collective-permute-start.1 = (f32[3,512]{1,0:T(4,128)S(1)}, f32[3,512]{1,0:T(4,128)S(1)}, u32[]{:S(2)}, u32[]{:S(2)}) collective-permute-start(f32[3,512]{1,0:T(4,128)S(1)} %get-tuple-element.1085), channel_id=1, source_target_pairs={{0,1},{1,2},{2,3},{3,4},{4,5},{5,6},{6,7},{7,8},{8,9},{9,10},{10,1... | collective-permute-start | bytes 18440 | tf_op jit(solution)/shard_map/ppermute | solution.py:26
  8.6 75.2 %collective-permute-start.3 = (f32[3,512]{1,0:T(4,128)S(1)}, f32[3,512]{1,0:T(4,128)S(1)}, u32[]{:S(2)}, u32[]{:S(2)}) collective-permute-start(f32[3,512]{1,0:T(4,128)S(1)} %get-tuple-element.1086), channel_id=1, source_target_pairs={{1,0},{2,1},{3,2},{4,3},{5,4},{6,5},{7,6},{8,7},{9,8},{10,9},{11,1... | collective-permute-start | bytes 18440 | tf_op jit(solution)/shard_map/ppermute | solution.py:28
  13.1 34.7 %copy-start.10 = (f32[128,5,1]{0,1,2:T(8,128)S(1)}, f32[128,5,1]{0,1,2:T(8,128)}, u32[]{:S(2)}) copy-start(f32[128,5,1]{0,1,2:T(8,128)} %constant.534) | copy-start | bytes 7684
  47.7 1.8 copy-start.9
  51.4 18.4 %copy-start.2 = (f32[128]{0:T(128)S(1)}, f32[128]{0:T(128)}, u32[]{:S(2)}) copy-start(f32[128]{0:T(128)} %constant.2011) | copy-start | bytes 1540
  51.4 18.4 %copy-start.4 = (f32[128]{0:T(128)S(1)}, f32[128]{0:T(128)}, u32[]{:S(2)}) copy-start(f32[128]{0:T(128)} %constant.489.clone..sunk.15) | copy-start | bytes 1540
  51.4 18.4 %copy-start.5 = (f32[128]{0:T(128)S(1)}, f32[128]{0:T(128)}, u32[]{:S(2)}) copy-start(f32[128]{0:T(128)} %constant.2010) | copy-start | bytes 1540
  51.4 18.4 %copy-start.6 = (f32[128]{0:T(128)S(1)}, f32[128]{0:T(128)}, u32[]{:S(2)}) copy-start(f32[128]{0:T(128)} %constant.490.clone..sunk.15) | copy-start | bytes 1540
  51.4 18.4 %copy-start.7 = (f32[128]{0:T(128)S(1)}, f32[128]{0:T(128)}, u32[]{:S(2)}) copy-start(f32[128]{0:T(128)} %constant.2009) | copy-start | bytes 1540
  69.9 13.5 %copy-start = (s32[16,9]{1,0:T(8,128)S(1)}, s32[16,9]{1,0:T(8,128)}, u32[]{:S(2)}) copy-start(s32[16,9]{1,0:T(8,128)} %param.28) | copy-start | bytes 1732
  69.9 13.8 %copy-start.1 = (f32[2048]{0:T(1024)S(1)}, f32[2048]{0:T(1024)}, u32[]{:S(2)}) copy-start(f32[2048]{0:T(1024)} %param.25) | copy-start | bytes 24580
  69.9 14.0 %copy-start.3 = (f32[3,2048]{1,0:T(4,128)S(1)}, f32[3,2048]{1,0:T(4,128)}, u32[]{:S(2)}) copy-start(f32[3,2048]{1,0:T(4,128)} %param.24) | copy-start | bytes 73732
  153.1 34.8 %collective-permute-start.4 = (f32[3,512]{1,0:T(4,128)S(1)}, f32[3,512]{1,0:T(4,128)S(1)}, u32[]{:S(2)}, u32[]{:S(2)}) collective-permute-start(f32[3,512]{1,0:T(4,128)S(1)} %get-tuple-element.1077), channel_id=1, source_target_pairs={{0,1},{1,2},{2,3},{3,4},{4,5},{5,6},{6,7},{7,8},{8,9},{9,10},{10,1... | collective-permute-start | bytes 18440 | tf_op jit(solution)/shard_map/ppermute | solution.py:26
  153.2 34.8 %collective-permute-start.5 = (f32[3,512]{1,0:T(4,128)S(1)}, f32[3,512]{1,0:T(4,128)S(1)}, u32[]{:S(2)}, u32[]{:S(2)}) collective-permute-start(f32[3,512]{1,0:T(4,128)S(1)} %get-tuple-element.1078), channel_id=1, source_target_pairs={{1,0},{2,1},{3,2},{4,3},{5,4},{6,5},{7,6},{8,7},{9,8},{10,9},{11,1... | collective-permute-start | bytes 18440 | tf_op jit(solution)/shard_map/ppermute | solution.py:28
  321.2 34.8 %collective-permute-start.6 = (f32[3,512]{1,0:T(4,128)S(1)}, f32[3,512]{1,0:T(4,128)S(1)}, u32[]{:S(2)}, u32[]{:S(2)}) collective-permute-start(f32[3,512]{1,0:T(4,128)S(1)} %get-tuple-element.1069), channel_id=1, source_target_pairs={{0,1},{1,2},{2,3},{3,4},{4,5},{5,6},{6,7},{7,8},{8,9},{9,10},{10,1... | collective-permute-start | bytes 18440 | tf_op jit(solution)/shard_map/ppermute | solution.py:26
  321.3 34.8 %collective-permute-start.7 = (f32[3,512]{1,0:T(4,128)S(1)}, f32[3,512]{1,0:T(4,128)S(1)}, u32[]{:S(2)}, u32[]{:S(2)}) collective-permute-start(f32[3,512]{1,0:T(4,128)S(1)} %get-tuple-element.1070), channel_id=1, source_target_pairs={{1,0},{2,1},{3,2},{4,3},{5,4},{6,5},{7,6},{8,7},{9,8},{10,9},{11,1... | collective-permute-start | bytes 18440 | tf_op jit(solution)/shard_map/ppermute | solution.py:28
where the time goes:
time: 434 us; the launch traced here: 428 us
  blocking collectives  237 us (55%)
  other arithmetic  145 us (33%)
  starting transfers between devices  19 us (4%)
  matrix products  13.6 us (3%)
  between operations  5.61 us (1%)
    reduce_sum x24, other arithmetic, near_tiles(): jnp.sum(weighted * delta_x - coef_three * moments[0][:, None, :], axis=2)  106 us
    psum x3, blocking collectives, moment(): return lax.psum(jnp.sum(values, axis=1), ('blk', 'oct', 'sub'))  90.8 us
    psum x2, blocking collectives, squares(): return lax.psum(jnp.sum(resid * scaled), ('blk', 'oct', 'sub'))  62.2 us
    all_gather x3, blocking collectives, induced(): piece = lax.all_gather(weights, ('blk', 'oct', 'sub'), axis=0, tiled=True)  52.3 us
    psum x1, blocking collectives, on_device(): lax.psum(jnp.sum(direction * image), ('blk', 'oct', 'sub'))  32 us
    reduce_sum x6, other arithmetic, far_block(): field_x = jnp.sum(weighted * delta_x - coef_three * weight_x, axis=(2, 3))  28.8 us
    ppermute x4, starting transfers between devices, padded(): lax.ppermute(head, axis, [((i + 1) % count, i) for i in range(count)])  18.3 us
  transfers between devices with their start and end apart: 8, of which 0 were waited for; matrix products, arithmetic and copies ran while one was open for 11% of the time, Pallas kernels for 0%

commit v1 on v0

--- a/solution.py
+++ b/solution.py
@@ -14,6 +14,12 @@
 layer_gap = 2.5
 thole_damp = 0.39
 highest = lax.Precision.HIGHEST
+
+
+def joined_along(blocks, dim):
+    shape = list(blocks.shape[1:])
+    shape[dim] *= blocks.shape[0]
+    return jnp.moveaxis(blocks, 0, dim).reshape(shape)
 
 
 def padded(cells, sides, width):
@@ -189,7 +195,14 @@
         weights = jnp.einsum(
             "pba,cba->bcp", interp, dipoles.reshape(3, BOXES_DEV, per_box), precision=highest
         )
-        piece = lax.all_gather(weights, ("blk", "oct", "sub"), axis=0, tiled=True)
+        size_2 = lax.axis_size(("blk", "oct", "sub"))
+        upward = [(i_2, (i_2 + 1) % size_2) for i_2 in range(size_2)]
+        blocks_2 = [weights]
+        while len(blocks_2) < size_2:
+            blocks_2.append(lax.ppermute(blocks_2[-1], ("blk", "oct", "sub"), upward))
+        index_2 = lax.axis_index(("blk", "oct", "sub"))
+        blocks_2 = jnp.stack(blocks_2)[(index_2 - jnp.arange(size_2)) % size_2]
+        piece = joined_along(blocks_2, 0)
         start = jnp.int32(0)
         count = piece.shape[0]
         size = split_size(count, group_limit)

time: 434 us -> 618 us (1.42)
  waiting for transfers between devices: 0.02 us -> 234 us
  blocking collectives: 237 us -> 183 us
    ppermute x0 -> x45, waiting for transfers between devices: none -> 230 us  [induced(): blocks_2.append(lax.ppermute(blocks_2[-1], ('blk', 'oct', 'sub'), upward))]
    all_gather x3 -> x0, blocking collectives: 52.3 us -> none  [induced(): piece = lax.all_gather(weights, ('blk', 'oct', 'sub'), axis=0, tiled=True)]
  transfers between devices with their start and end apart: 8 -> 53, of which waited for: 0 -> 42; matrix products, arithmetic and copies ran while one was open for 11% -> 19% of each run, Pallas kernels for 0% -> 0%
where the time goes in v1:
time: 618 us; the launch traced here: 612 us
  waiting for transfers between devices  234 us (38%)
  blocking collectives  183 us (30%)
  other arithmetic  144 us (23%)
  starting transfers between devices  20.2 us (3%)
  matrix products  13.6 us (2%)
  local copies, waits for them, and re-layouts  6.32 us (1%)
    ppermute x45, waiting for transfers between devices, induced(): blocks_2.append(lax.ppermute(blocks_2[-1], ('blk', 'oct', 'sub'), upward))  230 us
    reduce_sum x24, other arithmetic, near_tiles(): jnp.sum(weighted * delta_x - coef_three * moments[0][:, None, :], axis=2)  106 us
    psum x3, blocking collectives, moment(): return lax.psum(jnp.sum(values, axis=1), ('blk', 'oct', 'sub'))  92.9 us
    psum x2, blocking collectives, squares(): return lax.psum(jnp.sum(resid * scaled), ('blk', 'oct', 'sub'))  60.2 us
    psum x1, blocking collectives, on_device(): lax.psum(jnp.sum(direction * image), ('blk', 'oct', 'sub'))  30.1 us
    reduce_sum x6, other arithmetic, far_block(): field_x = jnp.sum(weighted * delta_x - coef_three * weight_x, axis=(2, 3))  28.8 us
    ppermute x4, starting transfers between devices, padded(): lax.ppermute(head, axis, [((i + 1) % count, i) for i in range(count)])  18.7 us
  transfers between devices with their start and end apart: 53, of which 42 were waited for; matrix products, arithmetic and copies ran while one was open for 19% of the time, Pallas kernels for 0%

profile of v1, /device:TPU:0, one launch (start us, length us, event | category | flops | bytes accessed | tf_op | source)
XLA Modules:
  0.0 611.6 jit_solution(12344325104021943435)
XLA Ops:
  22.6 33.9 %psum.49 = f32[3]{0:T(128)S(1)} all-reduce(f32[3]{0:T(128)S(1)} %get-tuple-element.927), channel_id=1, replica_groups=mesh['groups'=2,'blk'=4,'oct'=2,'sub'=2] {'blk','oct','sub'}, use_global_device_ids=true, to_apply=%region_33.34 | all-reduce | flops 3 | bytes 24 | tf_op jit(solution)/shard_map/psum | solution.py:223
  62.6 5.7 collective-permute-done.6
  92.9 7.3 %fusion.630 = (f32[16,128]{1,0:T(8,128)S(1)}, f32[16,128]{1,0:T(8,128)S(1)}, f32[16,128]{1,0:T(8,128)S(1)}, f32[16,128]{1,0:T(8,128)S(1)}, f32[16,128]{1,0:T(8,128)S(1)}, /*index=5*/f32[16,128]{1,0:T(8,128)S(1)}) fusion(f32[16,128]{1,0:T(8,128)S(1)} %bitcast.941, f32[16,128]{1,0:T(8,128)S(1)} %bitcast.848, f32[16,128]{1,0:T(8,128)S(1)} %bitcast.1028, ...), kind=kLoop, calls=%fused_computation.818 | loop fusion | flops 30920704 | bytes 180256 | tf_op jit(solution)/shard_map/reduce_sum | solution.py:76
  110.0 5.7 collective-permute-done.9
  115.7 5.7 collective-permute-done.10
  121.5 5.7 collective-permute-done.11
  127.2 5.7 collective-permute-done.12
  132.9 5.7 collective-permute-done.13
  138.7 5.7 collective-permute-done.14
  144.4 5.7 collective-permute-done.15
  150.1 5.7 collective-permute-done.16
  155.8 5.7 collective-permute-done.17
  161.6 5.7 collective-permute-done.18
  168.0 13.3 %while.51 = (s32[]{:T(128)}, f32[2,3,128]{2,0,1:T(2,128)S(1)}, s32[2]{0:T(128)S(1)}, f32[2,16,3,128]{3,1,2,0:T(8,128)S(1)}, s32[]{:T(128)}, /*index=5*/s32[]{:T(...) while((s32[]{:T(128)}, f32[2,3,128]{2,0,1:T(2,128)S(1)}, ...), condition=%wide.region_31.32_spmd.clone.clone.clone.clone, body=%wide.region_27.31_spmd.sunk.clone.clone.clone.clone.sunk | while | flops 16765948 | bytes 2795035 | solution.py:216
  182.4 29.5 %psum.51 = f32[3]{0:T(128)S(1)} all-reduce(f32[3]{0:T(128)S(1)} %get-tuple-element.923), channel_id=1, replica_groups=mesh['groups'=2,'blk'=4,'oct'=2,'sub'=2] {'blk','oct','sub'}, use_global_device_ids=true, to_apply=%region_69.70 | all-reduce | flops 3 | bytes 24 | tf_op jit(solution)/shard_map/psum | solution.py:223
  247.1 7.3 %fusion.629 = (f32[16,128]{1,0:T(8,128)S(1)}, f32[16,128]{1,0:T(8,128)S(1)}, f32[16,128]{1,0:T(8,128)S(1)}, f32[16,128]{1,0:T(8,128)S(1)}, f32[16,128]{1,0:T(8,128)S(1)}, /*index=5*/f32[16,128]{1,0:T(8,128)S(1)}) fusion(f32[16,128]{1,0:T(8,128)S(1)} %bitcast.978, f32[16,128]{1,0:T(8,128)S(1)} %bitcast.849, f32[16,128]{1,0:T(8,128)S(1)} %bitcast.1036, ...), kind=kLoop, calls=%fused_computation.817 | loop fusion | flops 30920704 | bytes 180256 | tf_op jit(solution)/shard_map/reduce_sum | solution.py:76
  264.2 5.7 collective-permute-done.24
  269.9 5.7 collective-permute-done.25
  275.7 5.7 collective-permute-done.26
  281.4 5.7 collective-permute-done.27
  287.1 5.7 collective-permute-done.28
  292.9 5.7 collective-permute-done.29
  298.6 5.7 collective-permute-done.30
  304.3 5.7 collective-permute-done.31
  310.1 5.7 collective-permute-done.32
  315.8 5.7 collective-permute-done.33
  321.5 5.7 collective-permute-done.34
  327.4 5.7 collective-permute-done.35
  333.7 13.3 %while.52 = (s32[]{:T(128)}, f32[2,3,128]{2,0,1:T(2,128)S(1)}, s32[2]{0:T(128)S(1)}, f32[2,16,3,128]{3,1,2,0:T(8,128)S(1)}, s32[]{:T(128)}, /*index=5*/s32[]{:T(...) while((s32[]{:T(128)}, f32[2,3,128]{2,0,1:T(2,128)S(1)}, ...), condition=%wide.region_67.68_spmd.clone.clone.clone.clone, body=%wide.region_63.67_spmd.sunk.clone.clone.clone.clone.sunk | while | flops 16765948 | bytes 2795035 | solution.py:216
  348.6 30.1 %all-reduce = (f32[]{:T(128)}, f32[]{:T(128)}) all-reduce(f32[]{:T(128)} %get-tuple-element.870, f32[]{:T(128)} %get-tuple-element.869), channel_id=1, replica_groups=mesh['groups'=2,'blk'=4,'oct'=2,'sub'=2] {'blk','oct','sub'}, use_global_device_ids=true, to_apply=%region_35.36 | all-reduce | flops 2 | bytes 16 | tf_op jit(solution)/shard_map/psum | solution.py:226
  380.7 30.1 %psum.53 = f32[]{:T(128)} all-reduce(f32[]{:T(128)} %fusion.632), channel_id=1, replica_groups=mesh['groups'=2,'blk'=4,'oct'=2,'sub'=2] {'blk','oct','sub'}, use_global_device_ids=true, to_apply=%region_73.74 | all-reduce | flops 1 | bytes 8 | tf_op jit(solution)/shard_map/psum | solution.py:226
  417.1 29.5 %psum.54 = f32[3]{0:T(128)S(1)} all-reduce(f32[3]{0:T(128)S(1)} %get-tuple-element.918), channel_id=1, replica_groups=mesh['groups'=2,'blk'=4,'oct'=2,'sub'=2] {'blk','oct','sub'}, use_global_device_ids=true, to_apply=%region_107.108 | all-reduce | flops 3 | bytes 24 | tf_op jit(solution)/shard_map/psum | solution.py:223
  447.2 5.7 collective-permute-done.38
  477.1 7.3 %fusion.628 = (f32[16,128]{1,0:T(8,128)S(1)}, f32[16,128]{1,0:T(8,128)S(1)}, f32[16,128]{1,0:T(8,128)S(1)}, f32[16,128]{1,0:T(8,128)S(1)}, f32[16,128]{1,0:T(8,128)S(1)}, /*index=5*/f32[16,128]{1,0:T(8,128)S(1)}) fusion(f32[16,128]{1,0:T(8,128)S(1)} %bitcast.969, f32[16,128]{1,0:T(8,128)S(1)} %bitcast.850, f32[16,128]{1,0:T(8,128)S(1)} %bitcast.1044, ...), kind=kLoop, calls=%fused_computation.816 | loop fusion | flops 30920704 | bytes 180256 | tf_op jit(solution)/shard_map/reduce_sum | solution.py:76
  488.5 5.7 collective-permute-done.40
  494.2 5.7 collective-permute-done.41
  499.9 5.7 collective-permute-done.42
  505.7 5.7 collective-permute-done.43
  511.4 5.7 collective-permute-done.44
  517.1 5.7 collective-permute-done.45
  522.9 5.7 collective-permute-done.46
  528.6 5.7 collective-permute-done.47
  534.3 5.7 collective-permute-done.48
  540.0 5.7 collective-permute-done.49
  545.8 5.7 collective-permute-done.50
  551.5 5.7 collective-permute-done.51
  563.8 13.1 %while.53 = (s32[]{:T(128)}, f32[2,3,128]{2,0,1:T(2,128)S(1)}, s32[2]{0:T(128)S(1)}, f32[2,16,3,128]{3,1,2,0:T(8,128)S(1)}, s32[]{:T(128)}, /*index=5*/s32[]{:T(...) while((s32[]{:T(128)}, f32[2,3,128]{2,0,1:T(2,128)S(1)}, ...), condition=%wide.region_105.106_spmd.clone.clone.clone.clone, body=%wide.region_101.105_spmd.sunk.clone.clone.clone.clone.sunk | while | flops 16765948 | bytes 2795035 | solution.py:216
  578.5 30.1 %psum.55 = f32[]{:T(128)} all-reduce(f32[]{:T(128)} %get-tuple-element.1110), channel_id=1, replica_groups=mesh['groups'=2,'blk'=4,'oct'=2,'sub'=2] {'blk','oct','sub'}, use_global_device_ids=true, to_apply=%region_109.110 | all-reduce | flops 1 | bytes 8 | tf_op jit(solution)/shard_map/psum | solution.py:235
  (311 shorter events, 190.8 us)
Async XLA Ops:
  1.6 55.4 %collective-permute-start.3 = (f32[3,512]{1,0:T(4,128)S(1)}, f32[3,512]{1,0:T(4,128)S(1)}, u32[]{:S(2)}, u32[]{:S(2)}) collective-permute-start(f32[3,512]{1,0:T(4,128)S(1)} %get-tuple-element.1086), channel_id=1, source_target_pairs={{1,0},{2,1},{3,2},{4,3},{5,4},{6,5},{7,6},{8,7},{9,8},{10,9},{11,1... | collective-permute-start | bytes 18440 | tf_op jit(solution)/shard_map/ppermute | solution.py:34
  8.5 60.0 %collective-permute-start = (f32[5,512]{1,0:T(8,128)S(1)}, f32[5,512]{1,0:T(8,128)S(1)}, u32[]{:S(2)}, u32[]{:S(2)}) collective-permute-start(f32[5,512]{1,0:T(8,128)S(1)} %get-tuple-element.989), channel_id=1, source_target_pairs={{0,1},{1,2},{2,3},{3,4},{4,5},{5,6},{6,7},{7,8},{8,9},{9,10},{10,1... | collective-permute-start | bytes 30728 | tf_op jit(solution)/shard_map/ppermute | solution.py:32
  8.6 60.0 %collective-permute-start.2 = (f32[5,512]{1,0:T(8,128)S(1)}, f32[5,512]{1,0:T(8,128)S(1)}, u32[]{:S(2)}, u32[]{:S(2)}) collective-permute-start(f32[5,512]{1,0:T(8,128)S(1)} %get-tuple-element.990), channel_id=1, source_target_pairs={{1,0},{2,1},{3,2},{4,3},{5,4},{6,5},{7,6},{8,7},{9,8},{10,9},{11,1... | collective-permute-start | bytes 30728 | tf_op jit(solution)/shard_map/ppermute | solution.py:34
  13.0 43.9 %collective-permute-start.1 = (f32[3,512]{1,0:T(4,128)S(1)}, f32[3,512]{1,0:T(4,128)S(1)}, u32[]{:S(2)}, u32[]{:S(2)}) collective-permute-start(f32[3,512]{1,0:T(4,128)S(1)} %get-tuple-element.1085), channel_id=1, source_target_pairs={{0,1},{1,2},{2,3},{3,4},{4,5},{5,6},{6,7},{7,8},{8,9},{9,10},{10,1... | collective-permute-start | bytes 18440 | tf_op jit(solution)/shard_map/ppermute | solution.py:32
  22.5 34.4 %collective-permute-start.4 = (f32[2,3,128]{2,1,0:T(4,128)S(1)}, f32[2,3,128]{2,1,0:T(4,128)S(1)}, u32[]{:S(2)}, u32[]{:S(2)}) collective-permute-start(f32[2,3,128]{2,1,0:T(4,128)S(1)} %get-tuple-element.1103), channel_id=1, source_target_pairs={{0,1},{1,2},{2,3},{3,4},{4,5},{5,6},{6,7},{7,8},{8,9},{9,10},{10,1... | collective-permute-start | bytes 9224 | tf_op jit(solution)/shard_map/ppermute | solution.py:202
  56.8 5.8 collective-permute-start.5
  62.6 5.7 collective-permute-start.6
  68.4 35.8 %collective-permute-start.7 = (f32[2,3,128]{2,1,0:T(4,128)S(1)}, f32[2,3,128]{2,1,0:T(4,128)S(1)}, u32[]{:S(2)}, u32[]{:S(2)}) collective-permute-start(f32[2,3,128]{2,1,0:T(4,128)S(1)} %collective-permute-done.6), channel_id=1, source_target_pairs={{0,1},{1,2},{2,3},{3,4},{4,5},{5,6},{6,7},{7,8},{8,9},{9,10},{10,1... | collective-permute-start | bytes 9224 | tf_op jit(solution)/shard_map/ppermute | solution.py:202
  104.2 5.8 collective-permute-start.8
  110.0 5.7 collective-permute-start.9
  115.7 5.7 collective-permute-start.10
  121.5 5.7 collective-permute-start.11
  127.2 5.7 collective-permute-start.12
  132.9 5.7 collective-permute-start.13
  138.6 5.7 collective-permute-start.14
  144.4 5.7 collective-permute-start.15
  150.1 5.7 collective-permute-start.16
  155.8 5.7 collective-permute-start.17
  161.6 5.7 collective-permute-start.18
  212.7 5.8 collective-permute-start.21
  212.8 6.1 %collective-permute-start.20 = (f32[3,512]{1,0:T(4,128)S(1)}, f32[3,512]{1,0:T(4,128)S(1)}, u32[]{:S(2)}, u32[]{:S(2)}) collective-permute-start(f32[3,512]{1,0:T(4,128)S(1)} %get-tuple-element.1078), channel_id=1, source_target_pairs={{1,0},{2,1},{3,2},{4,3},{5,4},{6,5},{7,6},{8,7},{9,8},{10,9},{11,1... | collective-permute-start | bytes 18440 | tf_op jit(solution)/shard_map/ppermute | solution.py:34
  217.2 5.8 collective-permute-start.19
  218.5 39.9 %collective-permute-start.22 = (f32[2,3,128]{2,1,0:T(4,128)S(1)}, f32[2,3,128]{2,1,0:T(4,128)S(1)}, u32[]{:S(2)}, u32[]{:S(2)}) collective-permute-start(f32[2,3,128]{2,1,0:T(4,128)S(1)} %collective-permute-done.21), channel_id=1, source_target_pairs={{0,1},{1,2},{2,3},{3,4},{4,5},{5,6},{6,7},{7,8},{8,9},{9,10},{10,1... | collective-permute-start | bytes 9224 | tf_op jit(solution)/shard_map/ppermute | solution.py:202
  258.4 5.8 collective-permute-start.23
  264.2 5.7 collective-permute-start.24
  269.9 5.7 collective-permute-start.25
  275.7 5.7 collective-permute-start.26
  281.4 5.7 collective-permute-start.27
  287.1 5.7 collective-permute-start.28
  292.9 5.7 collective-permute-start.29
  327.2 5.9 collective-permute-start.35
  412.6 40.4 %collective-permute-start.36 = (f32[3,512]{1,0:T(4,128)S(1)}, f32[3,512]{1,0:T(4,128)S(1)}, u32[]{:S(2)}, u32[]{:S(2)}) collective-permute-start(f32[3,512]{1,0:T(4,128)S(1)} %get-tuple-element.1069), channel_id=1, source_target_pairs={{0,1},{1,2},{2,3},{3,4},{4,5},{5,6},{6,7},{7,8},{8,9},{9,10},{10,1... | collective-permute-start | bytes 18440 | tf_op jit(solution)/shard_map/ppermute | solution.py:32
  412.6 40.3 %collective-permute-start.37 = (f32[3,512]{1,0:T(4,128)S(1)}, f32[3,512]{1,0:T(4,128)S(1)}, u32[]{:S(2)}, u32[]{:S(2)}) collective-permute-start(f32[3,512]{1,0:T(4,128)S(1)} %get-tuple-element.1070), channel_id=1, source_target_pairs={{1,0},{2,1},{3,2},{4,3},{5,4},{6,5},{7,6},{8,7},{9,8},{10,9},{11,1... | collective-permute-start | bytes 18440 | tf_op jit(solution)/shard_map/ppermute | solution.py:34
  447.1 5.8 collective-permute-start.38
  452.9 35.5 %collective-permute-start.39 = (f32[2,3,128]{2,1,0:T(4,128)S(1)}, f32[2,3,128]{2,1,0:T(4,128)S(1)}, u32[]{:S(2)}, u32[]{:S(2)}) collective-permute-start(f32[2,3,128]{2,1,0:T(4,128)S(1)} %collective-permute-done.38), channel_id=1, source_target_pairs={{0,1},{1,2},{2,3},{3,4},{4,5},{5,6},{6,7},{7,8},{8,9},{9,10},{10,1... | collective-permute-start | bytes 9224 | tf_op jit(solution)/shard_map/ppermute | solution.py:202
  488.4 5.8 collective-permute-start.40
  494.2 5.7 collective-permute-start.41
  499.9 5.7 collective-permute-start.42
  505.7 5.7 collective-permute-start.43
  511.4 5.7 collective-permute-start.44
  517.1 5.7 collective-permute-start.45
  522.8 5.7 collective-permute-start.46
  528.6 5.7 collective-permute-start.47
  534.3 5.7 collective-permute-start.48
  540.0 5.7 collective-permute-start.49
  545.8 5.7 collective-permute-start.50
  551.5 5.7 collective-permute-start.51
  557.2 5.9 collective-permute-start.52
  (17 other events, 526.5 us)
